TPU v7x, 32 devices: a whole 2x2x4 slice. The times are simulated.
32 devices in a mesh: groups: 2 (over y), ctx: 16 (over z, x, core).
Axes of the slice: x: 2, y: 2, z: 4, core: 2. Of those that a mesh axis runs over, the one named last changes fastest.
Arguments:
- queries: bfloat16 [12288, 1024], P(('groups', 'ctx')), parts along dimension 0, may hold values from -14 to 14
- inputs: bfloat16 [12288, 1024], P(('groups', 'ctx')), parts along dimension 0, may hold values from -6 to 6
- w_kv: bfloat16 [1024, 2048], replicated, may hold values from -1 to 1
- rand_blocks: int32 [192, 3], P('groups'), parts along dimension 0, may hold values from 1 to 94, as said below
- w_cross: bfloat16 [1024, 2048], replicated, may hold values from -1 to 1
- vocab_table: bfloat16 [6144, 1024], P('ctx'), may hold values from -14 to 14
- summary_ids: int32 [512], P('groups'), parts along dimension 0, may hold values from 0 to 6143
Outputs:
- attended: bfloat16 [12288, 1024], P(('groups', 'ctx')), parts along dimension 0
- summary: bfloat16 [512, 1024], P(('groups', 'ctx')), parts along dimension 0
There are 2 independent parts, one for each index of `groups`. A program takes and returns all parts, laid end to end along the dimension named above; an argument that names none is the same for every part. Nothing has to cross between parts.
Inputs may be any that keep to these rules, and one draw needn't show every extreme that they name: `rand_blocks`: take each run of 6 query blocks that starts at a multiple of 6: its 18 random blocks never lie in its own run (they may lie in any other run, and may repeat a block of the window), the 3 blocks of one query block lie in different runs, at most 2 of them lie in any one other run and some run holds exactly 2 of them. No random block is block 0 or block 95.
All inputs are finite; a program needn't handle non-finite values.
Results may differ from a plain program's by a relative error of at most 0.0075.
Values may be sent and summed in bfloat16 or wider, within the bound.
A program may use at most 192 MiB of HBM per device.

v0:
```python
import jax
import jax.numpy as jnp
from jax import lax
from jax.sharding import PartitionSpec as P

HEADS = 16
HEAD = 64
BLOCK = 64
MASKED_SCORE = -1e30


def from_root(block, axis, holder):
    block = jnp.where(lax.axis_index(axis) == holder, block, jnp.zeros_like(block))
    return lax.psum(block, axis)


def padded_2(x, sides, width):
    for axis, dim in sides:
        size, length = (lax.axis_size(axis), x.shape[dim])
        up = [(i, (i + 1) % size) for i in range(size - 1)]
        down = [(j, i) for i, j in up]
        last = lax.slice_in_dim(x, length - width, length, axis=dim)
        initial = lax.slice_in_dim(x, 0, width, axis=dim)
        before = lax.ppermute(last, axis, up)
        after = lax.ppermute(initial, axis, down)
        x = jnp.concatenate([before, x, after], axis=dim)
    return x


def partial_rows(query_rows, key_rows, value_rows):
    row_count = query_rows.shape[0]
    key_count = key_rows.shape[0]
    scores = jnp.einsum(
        "qhe,khe->qhk",
        query_rows.reshape(row_count, HEADS, HEAD),
        key_rows.reshape(key_count, HEADS, HEAD),
        preferred_element_type=jnp.float32,
    ) * HEAD ** (-0.5)
    peak = jnp.max(scores, axis=2)
    weights = jnp.exp(scores - peak[:, :, None])
    totals = jnp.sum(weights, axis=2)
    sums = jnp.einsum(
        "qhk,khe->qhe",
        weights,
        value_rows.reshape(key_count, HEADS, HEAD).astype(jnp.float32),
        precision=lax.Precision.HIGHEST,
    )
    return (peak, totals, sums.reshape(row_count, HEADS * HEAD))


def rescale(sums, scaling):
    row_count = sums.shape[0]
    return (sums.reshape(row_count, HEADS, HEAD) * scaling[:, :, None]).reshape(
        row_count, HEADS * HEAD
    )


def normalize(totals, sums):
    row_count = sums.shape[0]
    return (sums.reshape(row_count, HEADS, HEAD) / totals[:, :, None]).reshape(
        row_count, HEADS * HEAD
    )


def global_block(queries, key_value, root, start):
    query_piece = lax.slice_in_dim(queries, start, start + BLOCK, axis=0)
    pair_piece = lax.slice_in_dim(key_value, start, start + BLOCK, axis=0)
    return (from_root(query_piece, "ctx", root), from_root(pair_piece, "ctx", root))


def local(queries, inputs, w_kv, rand_blocks, w_cross, vocab_table, summary_ids):
    devices = lax.axis_size("ctx")
    position = lax.axis_index("ctx")
    row_count, feature_count = inputs.shape
    block_count = row_count // BLOCK
    pick_count = rand_blocks.shape[1]
    total_blocks = block_count * devices
    key_value = jnp.dot(inputs, w_kv, preferred_element_type=jnp.float32).astype(jnp.bfloat16)
    padded_inputs = padded_2(inputs, (("ctx", 0),), BLOCK)
    rim_rows = jnp.concatenate([padded_inputs[:BLOCK], padded_inputs[row_count + BLOCK :]], axis=0)
    rim_pairs = jnp.dot(rim_rows, w_kv, preferred_element_type=jnp.float32).astype(jnp.bfloat16)
    padded = jnp.concatenate([rim_pairs[:BLOCK], key_value, rim_pairs[BLOCK:]], axis=0)
    first_query, first_pair = global_block(queries, key_value, 0, 0)
    last_query, last_pair = global_block(queries, key_value, devices - 1, row_count - BLOCK)
    request_count = pick_count * block_count
    slot_count = (request_count + devices - 2) // (devices - 1)
    requests = rand_blocks.reshape(devices, request_count)
    owners = requests // block_count
    within = requests % block_count
    order = jnp.arange(request_count, dtype=jnp.int32)
    earlier = order[None, :] < order[:, None]
    matching = owners[:, :, None] == owners[:, None, :]
    ranks = jnp.sum(jnp.logical_and(matching, earlier[None, :, :]), axis=2)
    slot_ids = jnp.arange(slot_count, dtype=jnp.int32)
    served = jnp.logical_and(
        (owners == position)[:, None, :], ranks[:, None, :] == slot_ids[None, :, None]
    )
    sources = jnp.sum(jnp.where(served, within[:, None, :], 0), axis=2)
    filled = jnp.any(served, axis=2)
    outgoing = inputs.reshape(block_count, BLOCK, feature_count)[sources]
    outgoing = jnp.where(filled[:, :, None, None], outgoing, jnp.zeros((), jnp.bfloat16))
    arrived = lax.all_to_all(outgoing, "ctx", split_axis=0, concat_axis=0, tiled=True)
    my_owners = lax.dynamic_index_in_dim(owners, position, 0, keepdims=False)
    my_ranks = lax.dynamic_index_in_dim(ranks, position, 0, keepdims=False)
    fetched = arrived.reshape(devices * slot_count, BLOCK, feature_count)[
        my_owners * slot_count + my_ranks
    ]
    far_pairs = jnp.dot(
        fetched.reshape(request_count * BLOCK, feature_count),
        w_kv,
        preferred_element_type=jnp.float32,
    ).astype(jnp.bfloat16)
    far_pairs = far_pairs.reshape(block_count, pick_count * BLOCK, 2 * feature_count)
    framed = padded.reshape(block_count + 2, BLOCK, 2 * feature_count)
    window = jnp.concatenate(
        [framed[:block_count], framed[1 : block_count + 1], framed[2:]], axis=1
    )
    end_pairs = jnp.concatenate([first_pair, last_pair], axis=0)
    end_pairs = jnp.broadcast_to(end_pairs[None], (block_count, 2 * BLOCK, 2 * feature_count))
    key_sets = jnp.concatenate([window, end_pairs, far_pairs], axis=1)
    span = key_sets.shape[1]
    numbers = position * block_count + jnp.arange(block_count, dtype=jnp.int32)
    flags = jnp.stack(
        [numbers >= 2, jnp.ones((block_count,), dtype=bool), numbers <= total_blocks - 3], axis=1
    )
    valid = jnp.concatenate(
        [jnp.repeat(flags, BLOCK, axis=1), jnp.ones((block_count, span - 3 * BLOCK), dtype=bool)],
        axis=1,
    )
    query_blocks = queries.reshape(block_count, BLOCK, HEADS, HEAD)
    key_blocks = key_sets[:, :, :feature_count].reshape(block_count, span, HEADS, HEAD)
    value_blocks = key_sets[:, :, feature_count:].reshape(block_count, span, HEADS, HEAD)
    scores = jnp.einsum(
        "bqhe,bkhe->bhqk", query_blocks, key_blocks, preferred_element_type=jnp.float32
    ) * HEAD ** (-0.5)
    scores = jnp.where(valid[:, None, None, :], scores, MASKED_SCORE)
    weights = jnp.exp(scores - jnp.max(scores, axis=3, keepdims=True))
    probs = (weights / jnp.sum(weights, axis=3, keepdims=True)).astype(jnp.bfloat16)
    sparse_out = jnp.einsum(
        "bhqk,bkhe->bqhe", probs, value_blocks, preferred_element_type=jnp.float32
    )
    sparse_out = sparse_out.reshape(block_count, BLOCK, feature_count)
    end_queries = jnp.concatenate([first_query, last_query], axis=0)
    end_peak, end_totals, end_sums = partial_rows(
        end_queries, key_value[:, :feature_count], key_value[:, feature_count:]
    )
    shard_rows = vocab_table.shape[0]
    offsets = summary_ids - position * shard_rows
    inside = jnp.logical_and(offsets >= 0, offsets < shard_rows)
    looked = vocab_table[jnp.clip(offsets, 0, shard_rows - 1)].astype(jnp.float32)
    looked = jnp.where(inside[:, None], looked, 0.0)
    end_top = lax.pmax(end_peak, "ctx")
    end_scale = jnp.exp(end_peak - end_top)
    global_sums, global_totals, gathered_rows = lax.psum(
        (rescale(end_sums, end_scale), end_totals * end_scale, looked), "ctx"
    )
    global_out = normalize(global_totals, global_sums)
    sparse_out = sparse_out.at[0].set(jnp.where(position == 0, global_out[:BLOCK], sparse_out[0]))
    sparse_out = sparse_out.at[block_count - 1].set(
        jnp.where(position == devices - 1, global_out[BLOCK:], sparse_out[block_count - 1])
    )
    attended = sparse_out.reshape(row_count, feature_count).astype(jnp.bfloat16)
    encoded = (inputs.astype(jnp.float32) + attended.astype(jnp.float32)).astype(jnp.bfloat16)
    cross = jnp.dot(encoded, w_cross, preferred_element_type=jnp.float32).astype(jnp.bfloat16)
    summary_queries = gathered_rows.astype(jnp.bfloat16)
    cross_peak, cross_totals, cross_sums = partial_rows(
        summary_queries, cross[:, :feature_count], cross[:, feature_count:]
    )
    share = summary_queries.shape[0] // devices
    top_scores = lax.pmax(cross_peak, "ctx")
    scaling = jnp.exp(cross_peak - top_scores)
    scaled_sums = rescale(cross_sums, scaling)
    whole_sums, whole_totals = lax.psum((scaled_sums, cross_totals * scaling), "ctx")
    summary = lax.dynamic_slice_in_dim(
        normalize(whole_totals, whole_sums), position * share, share, 0
    )
    return (attended, summary.astype(jnp.bfloat16))


def solution(mesh):
    return jax.shard_map(
        local,
        mesh=mesh,
        in_specs=(
            P(("groups", "ctx"), None),
            P(("groups", "ctx"), None),
            P(),
            P("groups", None),
            P(),
            P("ctx", None),
            P("groups"),
        ),
        out_specs=(P(("groups", "ctx"), None), P(("groups", "ctx"), None)),
        check_vma=False,
    )
```

profile of v0, /device:TPU:0, one launch (start us, length us, event | category | flops | bytes accessed | tf_op | source)
XLA Modules:
  0.0 558.2 jit_solution(12927445662915458482)
XLA Ops:
  10.4 3.9 gather_fusion
  14.3 4.5 broadcast_select_fusion
  18.8 7.5 %all-to-all-start = ((bf16[16,2,64,1024]{3,2,1,0:T(8,128)(2,1)}), bf16[16,2,64,1024]{3,2,1,0:T(8,128)(2,1)}, u32[]{:S(2)}, u32[]{:S(2)}) async-start(bf16[16,2,64,1024]{3,2,1,0:T(8,128)(2,1)} %broadcast_select_fusion), calls=%async_computation | async-start | bytes 8388608 | tf_op jit(solution)/shard_map/all_to_all | solution.py:102
  27.0 2.3 collective-permute-start
  32.3 4.0 convolution_convert_fusion.2
  38.5 2.1 gather_fusion.2
  42.1 2.2 convert_select_fusion
  49.4 2.3 copy.111
  52.6 2.9 convolution_convert_fusion.3
  60.1 124.6 %all-reduce.12.cloned.1.call-done = (bf16[64,2048]{1,0:T(8,128)(2,1)}, bf16[64,2048]{1,0:T(8,128)(2,1)}, bf16[64,1024]{1,0:T(8,128)(2,1)}, bf16[64,1024]{1,0:T(8,128)(2,1)}) async-done(((bf16[64,2048]{1,0:T(8,128)(2,1)}, bf16[64,2048]{1,0:T(8,128)(2,1)}, bf16[64,1024]{1,0:T(8,128)(2,1)}, bf16[64,1024]{1,0:T(8,128)(2,1)}), (bf16[64,2048]{1,0:T(8,128)(2,1)}, bf16[64,2048]{1,0:T(8,128)(2,1)}, ...) | async-done | bytes 786448 | tf_op jit(solution)/shard_map/psum | solution.py:14
  185.9 2.3 bitcast_reduce_fusion.2
  188.2 30.9 %pmax.14 = f32[128,16]{0,1:T(8,128)S(1)} all-reduce(f32[128,16]{0,1:T(8,128)S(1)} %get-tuple-element.68), channel_id=1, replica_groups=mesh['groups'=2,'ctx'=16] {'ctx'}, use_global_device_ids=true, to_apply=%region_10.11 | all-reduce | flops 2048 | bytes 16384 | tf_op jit(solution)/shard_map/pmax | solution.py:152
  219.1 2.6 fusion.18
  222.0 2.5 fusion.39
  225.6 2.1 broadcast_dynamic-update-slice_fusion
  227.7 70.7 %all-reduce.13 = (f32[128,16]{0,1:T(8,128)S(1)}, bf16[256,1024]{1,0:T(8,128)(2,1)S(1)}) all-reduce(f32[128,16]{0,1:T(8,128)S(1)} %get-tuple-element.42, f32[256,1024]{1,0:T(8,128)S(1)} %copy-done.4), channel_id=1, replica_groups=mesh['groups'=2,'ctx'=16] {'ctx'}, use_global_device_ids=true, to_apply=%region_13.14 | all-reduce | flops 264192 | bytes 1589248 | tf_op jit(solution)/shard_map/psum | solution.py:154
  299.4 13.7 %all-reduce.8.cloned.1.call-done = f32[128,16,64]{0,2,1:T(8,128)} async-done(((f32[128,16,64]{0,2,1:T(8,128)}), f32[128,16,64]{0,2,1:T(8,128)}) %all-reduce.8.cloned.1.call-update) | async-done | bytes 524304 | tf_op jit(solution)/shard_map/psum | solution.py:154
  315.3 4.5 gather_fusion.1
  319.8 7.6 %convolution_convert_fusion = bf16[1152,2048]{1,0:T(8,128)(2,1)S(1)} fusion(bf16[1152,1024]{1,0:T(8,128)(2,1)} %bitcast.106, bf16[1024,2048]{1,0:T(8,128)(2,1)} %param.13), kind=kOutput, calls=%fused_computation.10 | convolution fusion | flops 4834197504 | bytes 11272192 | tf_op jit(solution)/shard_map/dot_general | solution.py:108
  327.3 2.6 constant_dynamic-update-slice_fusion
  329.9 10.4 %fusion.61 = (bf16[6,512,1024]{2,1,0:T(8,128)(2,1)}, bf16[6,512,1024]{2,1,0:T(8,128)(2,1)}) fusion(bf16[6,512,2048]{2,1,0:T(8,128)(2,1)} %constant_dynamic-update-slice_fusion), kind=kLoop, calls=%fused_computation.103 | loop fusion | bytes 25165824 | tf_op jit(solution)/shard_map/slice | solution.py:131
  340.4 8.7 %copy.108 = bf16[6,512,1024]{1,2,0:T(8,128)(2,1)} copy(bf16[6,512,1024]{2,1,0:T(8,128)(2,1)} %get-tuple-element.46) | data formatting | bytes 12582912 | tf_op jit(solution)/shard_map/slice | solution.py:131
  349.0 8.8 %copy.107 = bf16[6,512,1024]{1,2,0:T(8,128)(2,1)} copy(bf16[6,512,1024]{2,1,0:T(8,128)(2,1)} %get-tuple-element.47) | data formatting | bytes 12582912 | tf_op jit(solution)/shard_map/slice | solution.py:132
  357.8 11.1 %fusion.67 = (f32[6,16,64]{2,1,0:T(8,128)S(1)}, f32[6,16,64,512]{3,2,1,0:T(8,128)}) fusion(pred[6,512]{1,0:T(8,128)(4,1)S(1)} %concatenate.31, bf16[6,512,16,64]{1,3,2,0:T(8,128)(2,1)} %bitcast.95, bf16[6,64,16,64]{3,2,1,0:T(8,128)(2,1)S(1)} %copy-done.7), kind=kOutput, calls=%fused_computation.109 | convolution fusion | flops 415236608 | bytes 19688448 | tf_op jit(solution)/shard_map/sub | solution.py:137
  368.9 8.3 %fusion.8 = bf16[6,16,64,64]{3,2,1,0:T(8,128)(2,1)S(1)} fusion(bf16[6,512,16,64]{1,3,2,0:T(8,128)(2,1)} %bitcast.96, f32[6,16,64,512]{3,2,1,0:T(8,128)} %get-tuple-element.67, f32[6,16,64]{2,1,0:T(8,128)S(1)} %get-tuple-element.66), kind=kOutput, calls=%fused_computation.16 | convolution fusion | flops 408944640 | bytes 19685376 | tf_op jit(solution)/shard_map/bhqk,bkhe->bqhe/dot_general | solution.py:139
  379.2 4.3 convolution_convert_fusion.1
  384.5 3.7 bitcast_reduce_fusion.1
  388.2 59.0 %pmax.15 = f32[256,16]{0,1:T(8,128)S(1)} all-reduce(f32[256,16]{0,1:T(8,128)S(1)} %get-tuple-element.70), channel_id=1, replica_groups=mesh['groups'=2,'ctx'=16] {'ctx'}, use_global_device_ids=true, to_apply=%region_16.17 | all-reduce | flops 4096 | bytes 32768 | tf_op jit(solution)/shard_map/pmax | solution.py:170
  447.3 3.8 fusion.10
  451.5 7.1 %fusion.33 = f32[256,16,64]{0,2,1:T(8,128)} fusion(bf16[384,16,64]{0,2,1:T(8,128)(2,1)S(1)} %bitcast.104, f32[16,384,256]{2,1,0:T(8,128)} %get-tuple-element.71, f32[256,16]{0,1:T(8,128)S(1)} %get-tuple-element.70, f32[256,16]{0,1:T(8,128)S(1)} %get-tuple-element.41), kind=kOutput, calls=%fused_computation.42 | convolution fusion | flops 1211367424 | bytes 8159232 | tf_op jit(solution)/shard_map/qhk,khe->qhe/dot_general | solution.py:42
  458.7 57.9 %psum.71 = f32[256,16]{0,1:T(8,128)S(1)} all-reduce(f32[256,16]{0,1:T(8,128)S(1)} %get-tuple-element.40), channel_id=1, replica_groups=mesh['groups'=2,'ctx'=16] {'ctx'}, use_global_device_ids=true, to_apply=%region_19.20 | all-reduce | flops 4096 | bytes 32768 | tf_op jit(solution)/shard_map/psum | solution.py:173
  516.6 32.9 %all-reduce.10.cloned.1.call-done = f32[256,1024]{0,1:T(8,128)} async-done(((f32[256,1024]{0,1:T(8,128)}), f32[256,1024]{0,1:T(8,128)}) %all-reduce.10.cloned.1.call-update) | async-done | bytes 1048592 | tf_op jit(solution)/shard_map/psum | solution.py:173
  (98 shorter events, 32.5 us)
Async XLA Ops:
  7.2 31.3 %copy-start = (bf16[384,1024]{1,0:T(8,128)(2,1)S(1)}, bf16[384,1024]{1,0:T(8,128)(2,1)}, u32[]{:S(2)}) copy-start(bf16[384,1024]{1,0:T(8,128)(2,1)} %param.16) | copy-start | bytes 2359300
  18.8 7.6 %copy-start.3 = (bf16[384,1024]{1,0:T(8,128)(2,1)S(1)}, bf16[384,1024]{1,0:T(8,128)(2,1)}, u32[]{:S(2)}) copy-start(bf16[384,1024]{1,0:T(8,128)(2,1)} %param.12) | copy-start | bytes 2359300
  18.8 296.5 %all-to-all-start = ((bf16[16,2,64,1024]{3,2,1,0:T(8,128)(2,1)}), bf16[16,2,64,1024]{3,2,1,0:T(8,128)(2,1)}, u32[]{:S(2)}, u32[]{:S(2)}) async-start(bf16[16,2,64,1024]{3,2,1,0:T(8,128)(2,1)} %broadcast_select_fusion), calls=%async_computation | async-start | bytes 8388608 | tf_op jit(solution)/shard_map/all_to_all | solution.py:102
  26.3 158.3 %all-reduce.12.cloned.1.call-start = ((), (), s32[]{:S(2)}) async-start(), calls=%async_computation.3 | async-start | bytes 1572864 | tf_op jit(solution)/shard_map/psum | solution.py:14
  27.0 25.6 %collective-permute-start = (bf16[64,1024]{1,0:T(8,128)(2,1)}, bf16[64,1024]{1,0:T(8,128)(2,1)S(1)}, u32[]{:S(2)}, u32[]{:S(2)}) collective-permute-start(bf16[64,1024]{1,0:T(8,128)(2,1)} %get-tuple-element.58), channel_id=1, source_target_pairs={{0,1},{1,2},{2,3},{3,4},{4,5},{5,6},{6,7},{7,8},{8,9},{9,10},{10,1... | collective-permute-start | bytes 393224 | tf_op jit(solution)/shard_map/ppermute | solution.py:24
  29.3 23.3 %collective-permute-start.1 = (bf16[64,1024]{1,0:T(8,128)(2,1)S(1)}, bf16[64,1024]{1,0:T(8,128)(2,1)S(1)}, u32[]{:S(2)}, u32[]{:S(2)}) collective-permute-start(bf16[64,1024]{1,0:T(8,128)(2,1)S(1)} %get-tuple-element.59), channel_id=1, source_target_pairs={{1,0},{2,1},{3,2},{4,3},{5,4},{6,5},{7,6},{8,7},{9,8},{10,9},{11,1... | collective-permute-start | bytes 393224 | tf_op jit(solution)/shard_map/ppermute | solution.py:25
  37.2 276.0 %all-reduce.8.cloned.1.call-start = ((), (), s32[]{:S(2)}) async-start(), calls=%async_computation.1 | async-start | bytes 1048576 | tf_op jit(solution)/shard_map/psum | solution.py:154
  40.6 5.5 copy-start.8
  46.0 6.5 %copy-start.11 = (s32[18]{0:T(128)S(1)}, s32[18]{0:T(128)}, u32[]{:S(2)}) copy-start(s32[18]{0:T(128)} %fusion.53) | copy-start | bytes 220
  184.7 37.1 %copy-start.5 = (bf16[384,1024]{0,1:T(8,128)(2,1)S(1)}, bf16[384,1024]{0,1:T(8,128)(2,1)}, u32[]{:S(2)}) copy-start(bf16[384,1024]{0,1:T(8,128)(2,1)} %copy.111) | copy-start | bytes 2359300
  219.1 2.8 copy-start.2
  219.1 5.4 copy-start.10
  222.0 5.7 %copy-start.4 = (f32[256,1024]{1,0:T(8,128)S(1)}, f32[256,1024]{1,0:T(8,128)}, u32[]{:S(2)}) copy-start(f32[256,1024]{1,0:T(8,128)} %convert_select_fusion) | copy-start | bytes 3145732
  224.5 324.9 %all-reduce.10.cloned.1.call-start = ((), (), s32[]{:S(2)}) async-start(), calls=%async_computation.2 | async-start | bytes 2097152 | tf_op jit(solution)/shard_map/psum | solution.py:173
  349.0 8.8 %copy-start.7 = (bf16[6,64,16,64]{3,2,1,0:T(8,128)(2,1)S(1)}, bf16[6,64,16,64]{3,2,1,0:T(8,128)(2,1)}, u32[]{:S(2)}) copy-start(bf16[6,64,16,64]{3,2,1,0:T(8,128)(2,1)} %reshape.293) | copy-start | bytes 2359300
  379.2 4.3 copy-start.9
  383.5 1.0 copy-start.6
  451.5 100.1 %copy-start.1 = (bf16[384,1024]{1,0:T(8,128)(2,1)S(1)}, bf16[384,1024]{1,0:T(8,128)(2,1)}, u32[]{:S(2)}) copy-start(bf16[384,1024]{1,0:T(8,128)(2,1)} %param.16) | copy-start | bytes 2359300
Sparse Core Ops, SparseCore 0:
  37.3 147.3 all-reduce.11
  224.6 88.4 all-reduce.7
  458.8 90.5 all-reduce.9
where the time goes:
time: 560 us; the launch traced here: 558 us
  blocking collectives  219 us (39%)
  waiting for transfers between devices  171 us (31%)
  local copies, waits for them, and re-layouts  62.3 us (11%)
  matrix products  53.8 us (10%)
  other arithmetic  26.9 us (5%)
  between operations  14.2 us (3%)
  starting transfers between devices  11.2 us (2%)
    psum x1, waiting for transfers between devices, from_root(): return lax.psum(block, axis)  125 us
    psum x1, blocking collectives, local(): lax.psum((rescale(end_sums, end_scale), end_totals * end_scale, looked),...  70.7 us
    pmax x1, blocking collectives, local(): top_scores = lax.pmax(cross_peak, 'ctx')  59 us
    psum x1, blocking collectives, local(): lax.psum((scaled_sums, cross_totals * scaling), 'ctx')  57.9 us
    psum x1, waiting for transfers between devices, local(): lax.psum((scaled_sums, cross_totals * scaling), 'ctx')  32.9 us
    pmax x1, blocking collectives, local(): end_top = lax.pmax(end_peak, 'ctx')  30.9 us
    slice x2, local copies, waits for them, and re-layouts, local(): key_sets[:, :, :feature_count].reshape(block_count, span, HEADS, HEAD)  19.1 us
    psum x1, waiting for transfers between devices, local(): lax.psum((rescale(end_sums, end_scale), end_totals * end_scale, looked),...  13.7 us
  transfers between devices with their start and end apart: 6, of which 3 were waited for; matrix products, arithmetic and copies ran while one was open for 8% of the time, Pallas kernels for 0%

commit v1 on v0

--- a/solution.py
+++ b/solution.py
@@ -9,9 +9,14 @@
 MASKED_SCORE = -1e30
 
 
+def mark_cycles_on_mesh(block_here, device_axis):
+    plain = lax.all_gather(block_here, axis_name=device_axis)
+    return jnp.sum(plain, axis=0)
+
+
 def from_root(block, axis, holder):
     block = jnp.where(lax.axis_index(axis) == holder, block, jnp.zeros_like(block))
-    return lax.psum(block, axis)
+    return mark_cycles_on_mesh(block, device_axis=axis)
 
 
 def padded_2(x, sides, width):

time: 560 us -> 640 us (1.14)
  blocking collectives: 219 us -> 292 us
  other arithmetic: 26.9 us -> 34.4 us
    all_gather x0 -> x4, waiting for transfers between devices: none -> 138 us  [mark_cycles_on_mesh(): plain = lax.all_gather(block_here, axis_name=device_axis)]
    psum x1 -> x0, waiting for transfers between devices: 125 us -> none  [from_root(): return lax.psum(block, axis)]
    psum x1, blocking collectives: 70.7 us -> 143 us  [local(): lax.psum((rescale(end_sums, end_scale), end_totals * end_scale, looked),...]
    psum x1, waiting for transfers between devices: 13.7 us -> 0.01 us  [local(): lax.psum((rescale(end_sums, end_scale), end_totals * end_scale, looked),...]
    reduce_sum x0 -> x4, other arithmetic: none -> 9.93 us  [mark_cycles_on_mesh(): return jnp.sum(plain, axis=0)]
  transfers between devices with their start and end apart: 6 -> 9, of which waited for: 3 -> 5; matrix products, arithmetic and copies ran while one was open for 8% -> 8% of each run, Pallas kernels for 0% -> 0%
where the time goes in v1:
time: 640 us; the launch traced here: 638 us
  blocking collectives  292 us (46%)
  waiting for transfers between devices  172 us (27%)
  local copies, waits for them, and re-layouts  61.6 us (10%)
  matrix products  55.2 us (9%)
  other arithmetic  34.4 us (5%)
  between operations  14.5 us (2%)
  starting transfers between devices  9.1 us (1%)
    psum x1, blocking collectives, local(): lax.psum((rescale(end_sums, end_scale), end_totals * end_scale, looked),...  143 us
    all_gather x4, waiting for transfers between devices, mark_cycles_on_mesh(): plain = lax.all_gather(block_here, axis_name=device_axis)  138 us
    pmax x1, blocking collectives, local(): top_scores = lax.pmax(cross_peak, 'ctx')  58.3 us
    psum x1, blocking collectives, local(): lax.psum((scaled_sums, cross_totals * scaling), 'ctx')  58.2 us
    psum x1, waiting for transfers between devices, local(): lax.psum((scaled_sums, cross_totals * scaling), 'ctx')  32.7 us
    pmax x1, blocking collectives, local(): end_top = lax.pmax(end_peak, 'ctx')  31.9 us
    slice x2, local copies, waits for them, and re-layouts, local(): key_sets[:, :, :feature_count].reshape(block_count, span, HEADS, HEAD)  19.3 us
  transfers between devices with their start and end apart: 9, of which 5 were waited for; matrix products, arithmetic and copies ran while one was open for 8% of the time, Pallas kernels for 0%

profile of v1, /device:TPU:0, one launch (start us, length us, event | category | flops | bytes accessed | tf_op | source)
XLA Modules:
  0.0 638.3 jit_solution(1760254359267304034)
XLA Ops:
  9.8 4.2 convolution_convert_fusion.2
  17.7 36.6 %all-gather.15.cloned.1.call-done = bf16[1024,1024]{1,0:T(8,128)(2,1)} async-done(((bf16[64,1024]{1,0:T(8,128)(2,1)}), bf16[1024,1024]{1,0:T(8,128)(2,1)}) %all-gather.15.cloned.1.call-update) | async-done | bytes 2097168 | tf_op jit(solution)/shard_map/all_gather | solution.py:13
  56.3 40.4 %all-gather.13.cloned.1.call-done = bf16[1024,1024]{1,0:T(8,128)(2,1)} async-done(((bf16[64,1024]{1,0:T(8,128)(2,1)}), bf16[1024,1024]{1,0:T(8,128)(2,1)}) %all-gather.13.cloned.1.call-update) | async-done | bytes 2097168 | tf_op jit(solution)/shard_map/all_gather | solution.py:13
  102.8 31.9 %pmax.14 = f32[128,16]{0,1:T(8,128)S(1)} all-reduce(f32[128,16]{0,1:T(8,128)S(1)} %get-tuple-element.66), channel_id=1, replica_groups=mesh['groups'=2,'ctx'=16] {'ctx'}, use_global_device_ids=true, to_apply=%region_10.11 | all-reduce | flops 2048 | bytes 16384 | tf_op jit(solution)/shard_map/pmax | solution.py:157
  134.8 2.6 fusion.18
  138.0 3.7 fusion.39
  145.1 2.7 gather_fusion
  147.8 4.5 broadcast_select_fusion
  152.3 4.5 all-to-all-start
  158.9 3.0 collective-permute-start
  169.6 3.2 reshape.293
  173.0 2.9 convolution_convert_fusion.3
  180.4 143.5 %all-reduce.9 = (f32[128,16]{0,1:T(8,128)S(1)}, bf16[256,1024]{1,0:T(8,128)(2,1)S(1)}) all-reduce(f32[128,16]{0,1:T(8,128)S(1)} %copy-done.7, f32[256,1024]{1,0:T(8,128)} %convert_select_fusion), channel_id=1, replica_groups=mesh['groups'=2,'ctx'=16] {'ctx'}, use_global_device_ids=true, to_apply=%region_13.14 | all-reduce | flops 264192 | bytes 1589248 | tf_op jit(solution)/shard_map/psum | solution.py:159
  327.1 12.2 %all-gather.11.cloned.1.call-done = bf16[1024,2048]{1,0:T(8,128)(2,1)} async-done(((bf16[64,2048]{1,0:T(8,128)(2,1)}), bf16[1024,2048]{1,0:T(8,128)(2,1)}) %all-gather.11.cloned.1.call-update) | async-done | bytes 4194320 | tf_op jit(solution)/shard_map/all_gather | solution.py:13
  339.3 3.0 reduce_sum.96
  342.3 48.4 %all-gather.9.cloned.1.call-done = bf16[1024,2048]{1,0:T(8,128)(2,1)} async-done(((bf16[64,2048]{1,0:T(8,128)(2,1)}), bf16[1024,2048]{1,0:T(8,128)(2,1)}) %all-gather.9.cloned.1.call-update) | async-done | bytes 4194320 | tf_op jit(solution)/shard_map/all_gather | solution.py:13
  390.7 3.0 reduce_sum.95
  393.7 4.5 gather_fusion.1
  398.2 7.6 %convolution_convert_fusion = bf16[1152,2048]{1,0:T(8,128)(2,1)S(1)} fusion(bf16[1152,1024]{1,0:T(8,128)(2,1)} %bitcast.112, bf16[1024,2048]{1,0:T(8,128)(2,1)} %param.13), kind=kOutput, calls=%fused_computation.10 | convolution fusion | flops 4834197504 | bytes 11272192 | tf_op jit(solution)/shard_map/dot_general | solution.py:113
  408.0 2.6 constant_dynamic-update-slice_fusion
  410.5 10.5 %fusion.61 = (bf16[6,512,1024]{2,1,0:T(8,128)(2,1)}, bf16[6,512,1024]{2,1,0:T(8,128)(2,1)}) fusion(bf16[6,512,2048]{2,1,0:T(8,128)(2,1)} %constant_dynamic-update-slice_fusion), kind=kLoop, calls=%fused_computation.103 | loop fusion | bytes 25165824 | tf_op jit(solution)/shard_map/slice | solution.py:136
  421.0 8.7 %copy.122 = bf16[6,512,1024]{1,2,0:T(8,128)(2,1)} copy(bf16[6,512,1024]{2,1,0:T(8,128)(2,1)} %get-tuple-element.45) | data formatting | bytes 12582912 | tf_op jit(solution)/shard_map/slice | solution.py:137
  429.7 8.8 %copy.123 = bf16[6,512,1024]{1,2,0:T(8,128)(2,1)} copy(bf16[6,512,1024]{2,1,0:T(8,128)(2,1)} %get-tuple-element.44) | data formatting | bytes 12582912 | tf_op jit(solution)/shard_map/slice | solution.py:136
  438.4 11.1 %fusion.67 = (f32[6,16,64]{2,1,0:T(8,128)S(1)}, f32[6,16,64,512]{3,2,1,0:T(8,128)}) fusion(pred[6,512]{1,0:T(8,128)(4,1)S(1)} %concatenate.31, bf16[6,512,16,64]{1,3,2,0:T(8,128)(2,1)} %bitcast.100, bf16[6,64,16,64]{3,2,1,0:T(8,128)(2,1)S(1)} %copy-done.5), kind=kOutput, calls=%fused_computation.109 | convolution fusion | flops 415236608 | bytes 19688448 | tf_op jit(solution)/shard_map/sub | solution.py:142
  449.5 8.3 %fusion.8 = bf16[6,16,64,64]{3,2,1,0:T(8,128)(2,1)S(1)} fusion(bf16[6,512,16,64]{1,3,2,0:T(8,128)(2,1)} %bitcast.99, f32[6,16,64,512]{3,2,1,0:T(8,128)} %get-tuple-element.65, f32[6,16,64]{2,1,0:T(8,128)S(1)} %get-tuple-element.64), kind=kOutput, calls=%fused_computation.16 | convolution fusion | flops 408944640 | bytes 19685376 | tf_op jit(solution)/shard_map/bhqk,bkhe->bqhe/dot_general | solution.py:144
  459.7 4.3 convolution_convert_fusion.1
  465.0 3.7 bitcast_reduce_fusion.1
  468.7 58.3 %pmax.15 = f32[256,16]{0,1:T(8,128)S(1)} all-reduce(f32[256,16]{0,1:T(8,128)S(1)} %get-tuple-element.68), channel_id=1, replica_groups=mesh['groups'=2,'ctx'=16] {'ctx'}, use_global_device_ids=true, to_apply=%region_16.17 | all-reduce | flops 4096 | bytes 32768 | tf_op jit(solution)/shard_map/pmax | solution.py:175
  526.9 3.8 fusion.10
  531.2 7.2 %fusion.33 = f32[256,16,64]{0,2,1:T(8,128)} fusion(bf16[384,16,64]{0,2,1:T(8,128)(2,1)S(1)} %bitcast.110, f32[16,384,256]{2,1,0:T(8,128)} %get-tuple-element.69, f32[256,16]{0,1:T(8,128)S(1)} %get-tuple-element.68, f32[256,16]{0,1:T(8,128)S(1)} %get-tuple-element.39), kind=kOutput, calls=%fused_computation.42 | convolution fusion | flops 1211367424 | bytes 8159232 | tf_op jit(solution)/shard_map/qhk,khe->qhe/dot_general | solution.py:47
  538.4 58.2 %psum.39 = f32[256,16]{0,1:T(8,128)S(1)} all-reduce(f32[256,16]{0,1:T(8,128)S(1)} %get-tuple-element.38), channel_id=1, replica_groups=mesh['groups'=2,'ctx'=16] {'ctx'}, use_global_device_ids=true, to_apply=%region_19.20 | all-reduce | flops 4096 | bytes 32768 | tf_op jit(solution)/shard_map/psum | solution.py:178
  596.5 32.7 %all-reduce.8.cloned.1.call-done = f32[256,1024]{0,1:T(8,128)} async-done(((f32[256,1024]{0,1:T(8,128)}), f32[256,1024]{0,1:T(8,128)}) %all-reduce.8.cloned.1.call-update) | async-done | bytes 1048592 | tf_op jit(solution)/shard_map/psum | solution.py:178
  (105 shorter events, 43.4 us)
Async XLA Ops:
  7.2 156.7 %copy-start = (bf16[384,1024]{1,0:T(8,128)(2,1)S(1)}, bf16[384,1024]{1,0:T(8,128)(2,1)}, u32[]{:S(2)}) copy-start(bf16[384,1024]{1,0:T(8,128)(2,1)} %param.16) | copy-start | bytes 2359300
  7.2 47.1 %all-gather.15.cloned.1.call-start = ((), (), s32[]{:S(2)}) async-start(), calls=%async_computation.6 | async-start | bytes 2228224 | tf_op jit(solution)/shard_map/all_gather | solution.py:13
  9.0 87.6 %all-gather.13.cloned.1.call-start = ((), (), s32[]{:S(2)}) async-start(), calls=%async_computation.5 | async-start | bytes 2228224 | tf_op jit(solution)/shard_map/all_gather | solution.py:13
  9.8 315.2 %all-reduce.6.cloned.1.call-start = ((), (), s32[]{:S(2)}) async-start(), calls=%async_computation.1 | async-start | bytes 1048576 | tf_op jit(solution)/shard_map/psum | solution.py:159
  134.8 3.2 copy-start.2
  134.8 8.4 %copy-start.8 = (s32[96,3]{0,1:T(4,128)S(1)}, s32[96,3]{0,1:T(4,128)}, u32[]{:S(2)}) copy-start(s32[96,3]{0,1:T(4,128)} %param.14) | copy-start | bytes 3460
  137.4 7.7 %copy-start.3 = (bf16[384,1024]{1,0:T(8,128)(2,1)S(1)}, bf16[384,1024]{1,0:T(8,128)(2,1)}, u32[]{:S(2)}) copy-start(bf16[384,1024]{1,0:T(8,128)(2,1)} %param.12) | copy-start | bytes 2359300
  141.7 197.6 %all-gather.11.cloned.1.call-start = ((), (), s32[]{:S(2)}) async-start(), calls=%async_computation.4 | async-start | bytes 4456448 | tf_op jit(solution)/shard_map/all_gather | solution.py:13
  142.6 248.1 %all-gather.9.cloned.1.call-start = ((), (), s32[]{:S(2)}) async-start(), calls=%async_computation.3 | async-start | bytes 4456448 | tf_op jit(solution)/shard_map/all_gather | solution.py:13
  152.3 241.4 %all-to-all-start = ((bf16[16,2,64,1024]{3,2,1,0:T(8,128)(2,1)}), bf16[16,2,64,1024]{3,2,1,0:T(8,128)(2,1)}, u32[]{:S(2)}, u32[]{:S(2)}) async-start(bf16[16,2,64,1024]{3,2,1,0:T(8,128)(2,1)} %broadcast_select_fusion), calls=%async_computation | async-start | bytes 8388608 | tf_op jit(solution)/shard_map/all_to_all | solution.py:107
  156.9 472.4 %all-reduce.8.cloned.1.call-start = ((), (), s32[]{:S(2)}) async-start(), calls=%async_computation.2 | async-start | bytes 2097152 | tf_op jit(solution)/shard_map/psum | solution.py:178
  157.6 15.4 %collective-permute-start.1 = (bf16[64,1024]{1,0:T(8,128)(2,1)}, bf16[64,1024]{1,0:T(8,128)(2,1)S(1)}, u32[]{:S(2)}, u32[]{:S(2)}) collective-permute-start(bf16[64,1024]{1,0:T(8,128)(2,1)} %get-tuple-element.57), channel_id=1, source_target_pairs={{1,0},{2,1},{3,2},{4,3},{5,4},{6,5},{7,6},{8,7},{9,8},{10,9},{11,1... | collective-permute-start | bytes 393224 | tf_op jit(solution)/shard_map/ppermute | solution.py:30
  158.9 14.1 %collective-permute-start = (bf16[64,1024]{1,0:T(8,128)(2,1)S(1)}, bf16[64,1024]{1,0:T(8,128)(2,1)S(1)}, u32[]{:S(2)}, u32[]{:S(2)}) collective-permute-start(bf16[64,1024]{1,0:T(8,128)(2,1)S(1)} %get-tuple-element.56), channel_id=1, source_target_pairs={{0,1},{1,2},{2,3},{3,4},{4,5},{5,6},{6,7},{7,8},{8,9},{9,10},{10,1... | collective-permute-start | bytes 393224 | tf_op jit(solution)/shard_map/ppermute | solution.py:29
  176.4 4.1 copy-start.7
  429.7 8.8 %copy-start.5 = (bf16[6,64,16,64]{3,2,1,0:T(8,128)(2,1)S(1)}, bf16[6,64,16,64]{3,2,1,0:T(8,128)(2,1)}, u32[]{:S(2)}) copy-start(bf16[6,64,16,64]{3,2,1,0:T(8,128)(2,1)} %reshape.293) | copy-start | bytes 2359300
  459.7 4.3 copy-start.6
  464.0 1.0 copy-start.4
  531.2 100.3 %copy-start.1 = (bf16[384,1024]{1,0:T(8,128)(2,1)S(1)}, bf16[384,1024]{1,0:T(8,128)(2,1)}, u32[]{:S(2)}) copy-start(bf16[384,1024]{1,0:T(8,128)(2,1)} %param.16) | copy-start | bytes 2359300
Sparse Core Ops, SparseCore 0:
  10.2 44.0 all-gather.14
  56.5 40.1 all-gather.12
  141.8 139.9 all-reduce.5
  283.8 55.4 all-gather.10
  341.3 49.3 all-gather.8
  538.5 90.7 all-reduce.7
